TPU v7x, 512 devices: a whole 4x4x16 slice. The times are simulated.
512 devices in a mesh: batch: 32 (over z, core), row: 4 (over y), col: 4 (over x).
Axes of the slice: x: 4, y: 4, z: 16, core: 2. Of those that a mesh axis runs over, the one named last changes fastest.
Arguments:
- image_tokens: bfloat16 [128, 256, 3072], P('batch', ('row', 'col')), may hold values from -36 to 36
- text_tokens: bfloat16 [128, 128, 3072], P('batch', ('row', 'col')), may hold values from -36 to 36
- modulation: float32 [128, 7, 3072], P('batch'), may hold values from -3.5 to 3.5
- qkv_weight: bfloat16 [3072, 12, 384], P('col', 'row'), may hold values from -0.109375 to 0.109375
- kv_weight: bfloat16 [3072, 12, 256], P('col', 'row'), may hold values from -0.109375 to 0.109375
- norm_gains: float32 [3, 128], replicated, may hold values from 1 to 2.2
- out_weight: bfloat16 [12, 128, 3072], P('row', None, 'col'), may hold values from -0.15625 to 0.15625
- final_weight: bfloat16 [3072, 64], replicated, may hold values from -0.109375 to 0.109375
- text_lengths: int32 [128], P('batch'), may hold values from 1 to 128, as said below
- partner: int32 [128], P('batch'), may hold values from 0 to 127, as said below
- guidance: float32 [128], P('batch'), may hold values from 1.5 to 4.5
- step_size: float32 [128], P('batch'), may hold values from -0.3 to -0.05
- latent: float32 [128, 256, 64], P('batch', ('row', 'col')), may hold values from -6 to 6
Outputs:
- next_latent: float32 [128, 256, 64], P('batch', ('row', 'col'))
Inputs may be any that keep to these rules, and one draw needn't show every extreme that they name: `text_lengths`: some sequence has all 128 text tokens live. partner[partner[s]] = s and partner[s] != s for every sequence s.
All inputs are finite; a program needn't handle non-finite values.
Results may differ from a plain program's by a relative error of at most 0.007.
Values may be sent and summed in bfloat16 or wider, within the bound.
No kernel may reach another device: no remote copies, remote signals or barrier semaphores. Data moves between devices by JAX's collectives and lax.ppermute only.
A program may use at most 64 MiB of HBM per device.

v0:
```python
import math
import jax
import jax.numpy as jnp
from jax import lax
from jax.sharding import PartitionSpec as P

epsilon = 1e-06


def layer_norm(values):
    center = jnp.mean(values, axis=-1, keepdims=True)
    spread = jnp.mean((values - center) * (values - center), axis=-1, keepdims=True)
    return (values - center) * lax.rsqrt(spread + epsilon)


def modulate(values, shift, scale):
    return layer_norm(values) * (1.0 + scale[:, None, :]) + shift[:, None, :]


def head_norm(values, gain):
    return values * lax.rsqrt(jnp.mean(values * values, axis=-1, keepdims=True) + epsilon) * gain


def attend(queries, all_keys, all_values, live, head_size):
    scores = jnp.einsum(
        "sqhe,skhe->shqk", queries, all_keys, preferred_element_type=jnp.float32
    ) / math.sqrt(head_size)
    expo = jnp.exp(scores) * live[:, None, None, :]
    totals = jnp.sum(expo, axis=-1)
    mixed = jnp.einsum(
        "shqk,skhe->sqhe", expo.astype(jnp.bfloat16), all_values, preferred_element_type=jnp.float32
    )
    return (mixed / jnp.transpose(totals, (0, 2, 1))[..., None]).astype(jnp.bfloat16)


def per_device(
    image_tokens,
    text_tokens,
    modulation,
    qkv_weight,
    kv_weight,
    norm_gains,
    out_weight,
    final_weight,
    text_lengths,
    partner,
    guidance,
    step_size,
    latent,
):
    count = image_tokens.shape[0]
    head_size = norm_gains.shape[1]
    block_width = qkv_weight.shape[0]
    image_mod = modulate(
        image_tokens.astype(jnp.float32), modulation[:, 0], modulation[:, 1]
    ).astype(jnp.bfloat16)
    text_mod = modulate(text_tokens.astype(jnp.float32), modulation[:, 3], modulation[:, 4]).astype(
        jnp.bfloat16
    )
    image_whole, text_whole = (
        lax.all_gather(image_mod, ("row", "col"), axis=1, tiled=True),
        lax.all_gather(text_mod, ("row", "col"), axis=1, tiled=True),
    )
    offset = lax.axis_index("col") * block_width
    image_all = lax.dynamic_slice_in_dim(image_whole, offset, block_width, 2)
    text_all = lax.dynamic_slice_in_dim(text_whole, offset, block_width, 2)
    qkv_term = jnp.einsum(
        "std,dhe->sthe", image_all, qkv_weight, preferred_element_type=jnp.float32
    )
    kv_term = jnp.einsum("std,dhe->sthe", text_all, kv_weight, preferred_element_type=jnp.float32)
    qkv_sum, kv_sum = (
        lax.psum(qkv_term.astype(jnp.bfloat16), "col").astype(jnp.float32),
        lax.psum(kv_term.astype(jnp.bfloat16), "col").astype(jnp.float32),
    )
    queries = head_norm(qkv_sum[..., :head_size], norm_gains[0]).astype(jnp.bfloat16)
    image_keys = head_norm(qkv_sum[..., head_size : 2 * head_size], norm_gains[1]).astype(
        jnp.bfloat16
    )
    image_values = qkv_sum[..., 2 * head_size :].astype(jnp.bfloat16)
    text_keys = head_norm(kv_sum[..., :head_size], norm_gains[2]).astype(jnp.bfloat16)
    text_values = kv_sum[..., head_size:].astype(jnp.bfloat16)
    text_count = text_keys.shape[1]
    image_count = image_keys.shape[1]
    all_keys = jnp.concatenate([text_keys, image_keys], axis=1)
    all_values = jnp.concatenate([text_values, image_values], axis=1)
    text_live = (jnp.arange(text_count, dtype=jnp.int32)[None, :] < text_lengths[:, None]).astype(
        jnp.float32
    )
    live = jnp.concatenate([text_live, jnp.ones((count, image_count), jnp.float32)], axis=1)
    heads = attend(queries, all_keys, all_values, live, head_size)
    out_term = jnp.einsum("sqhe,hed->sqd", heads, out_weight, preferred_element_type=jnp.float32)
    attn_rows = lax.psum_scatter(
        out_term.astype(jnp.bfloat16), "row", scatter_dimension=1, tiled=True
    )
    attn_tokens = lax.all_to_all(attn_rows, "col", split_axis=1, concat_axis=2, tiled=True)
    residual = image_tokens.astype(jnp.float32) + modulation[:, 2][:, None, :] * attn_tokens.astype(
        jnp.float32
    )
    final_in = modulate(residual, modulation[:, 5], modulation[:, 6]).astype(jnp.bfloat16)
    velocity = jnp.einsum("std,dc->stc", final_in, final_weight, preferred_element_type=jnp.float32)
    token_rows = velocity.shape[1]
    channels = velocity.shape[2]
    flat_velocity = velocity.reshape(count, token_rows * channels)
    every_velocity, every_guidance = (
        lax.all_gather(flat_velocity, "batch", axis=0, tiled=True),
        lax.all_gather(guidance, "batch", axis=0, tiled=True),
    )
    mate = jnp.take(every_velocity, partner, axis=0).reshape(velocity.shape)
    own_index = lax.axis_index("batch") * count + jnp.arange(count, dtype=jnp.int32)
    is_cond = own_index < partner
    cond_vel = jnp.where(is_cond[:, None, None], velocity, mate)
    uncond_vel = jnp.where(is_cond[:, None, None], mate, velocity)
    scale_guide = jnp.where(is_cond, guidance, jnp.take(every_guidance, partner))
    guided = uncond_vel + scale_guide[:, None, None] * (cond_vel - uncond_vel)
    ratio = jnp.sqrt(
        (jnp.mean(cond_vel * cond_vel, axis=-1, keepdims=True) + epsilon)
        / (jnp.mean(guided * guided, axis=-1, keepdims=True) + epsilon)
    )
    return latent + step_size[:, None, None] * guided * (0.7 * ratio + 0.3)


def solution(mesh):
    return jax.shard_map(
        per_device,
        mesh=mesh,
        in_specs=(
            P("batch", ("row", "col"), None),
            P("batch", ("row", "col"), None),
            P("batch", None, None),
            P("col", "row", None),
            P("col", "row", None),
            P(),
            P("row", None, "col"),
            P(),
            P("batch"),
            P("batch"),
            P("batch"),
            P("batch"),
            P("batch", ("row", "col"), None),
        ),
        out_specs=P("batch", ("row", "col"), None),
        check_vma=False,
    )
```

profile of v0, /device:TPU:1, one launch (start us, length us, event | category | flops | bytes accessed | tf_op | source)
XLA Modules:
  0.0 376.6 jit_solution(10970847019949007939)
XLA Ops:
  6.5 1.2 convert_reduce_fusion.1
  7.7 1.1 fusion.42
  8.9 1.0 slice_bitcast_fusion.3
  9.9 1.8 fusion.45
  11.7 1.1 convert_reduce_fusion
  13.1 1.0 fusion.30
  14.2 65.4 %all-gather.4.cloned.1.call-done = bf16[4,128,3072]{2,1,0:T(8,128)(2,1)} async-done(((bf16[4,8,3072]{2,1,0:T(8,128)(2,1)}), bf16[4,128,3072]{2,1,0:T(8,128)(2,1)}) %all-gather.4.cloned.1.call-update) | async-done | bytes 3145744 | tf_op jit(solution)/shard_map/all_gather | solution.py:62
  79.6 3.2 convolution_convert_fusion.1
  82.7 75.8 %all-gather.6.cloned.1.call-done = bf16[4,256,3072]{2,1,0:T(8,128)(2,1)} async-done(((bf16[4,16,3072]{2,1,0:T(8,128)(2,1)}), bf16[4,256,3072]{2,1,0:T(8,128)(2,1)}) %all-gather.6.cloned.1.call-update) | async-done | bytes 6291472 | tf_op jit(solution)/shard_map/all_gather | solution.py:61
  158.5 5.0 %convolution_convert_fusion = bf16[4,256,3,384]{3,1,2,0:T(8,128)(2,1)} fusion(bf16[768,3,384]{2,0,1:T(8,128)(2,1)S(1)} %copy-done, bf16[4,256,3072]{2,1,0:T(8,128)(2,1)} %all-gather.6.cloned.1.call-done, s32[]{:T(128)S(6)} %select_n.32), kind=kOutput, calls=%fused_computation.9 | convolution fusion | flops 1813118976 | bytes 5701636 | tf_op jit(solution)/shard_map/std,dhe->sthe/dot_general | solution.py:67
  163.6 0.6 copy-done.9
  164.3 90.3 %all-reduce.5.cloned.1.call-done = (bf16[4,256,3,384]{3,1,2,0:T(8,128)(2,1)}, bf16[4,128,3,256]{3,1,2,0:T(8,128)(2,1)}) async-done(((bf16[4,256,3,384]{3,1,2,0:T(8,128)(2,1)}, bf16[4,128,3,256]{3,1,2,0:T(8,128)(2,1)}), (bf16[4,256,3,384]{3,1,2,0:T(8,128)(2,1)}, bf16[4,128,3,256]{3,1,2,0:T(8,128)(2,1)})) %all-reduce.5.cloned.1.call-update) | async-done | bytes 3145744 | tf_op jit(solution)/shard_map/psum | solution.py:72
  254.6 1.4 fusion.31
  256.0 1.0 slice.70
  257.1 1.2 slice.71
  258.3 0.4 convert_element_type.65
  258.7 0.9 multiply_reduce_fusion.1
  260.2 0.5 multiply_convert_fusion
  260.6 2.8 fusion
  263.4 5.8 %bitcast_convert_fusion = bf16[4,256,768]{2,1,0:T(8,128)(2,1)} fusion(f32[4,3,256,384]{3,2,1,0:T(8,128)} %get-tuple-element.25, f32[4,384]{1,0:T(4,128)S(1)} %pad_convert_fusion, bf16[4,256,3,128]{3,1,2,0:T(8,128)(2,1)S(1)} %slice.71, bf16[4,128,3,128]{3,1,2,0:T(8,128)(2,1)S(1)} %slice.70, f32[4,256,3]{1,2,0:T(4,128)S(1)} %bitcast.60, ...), kind=kOutput, calls=%fused_computation.5 | convolution fusion | flops 913440768 | bytes 8079360 | tf_op jit(solution)/shard_map/sqhe,hed->sqd/dot_general | solution.py:91
  269.2 1.3 dynamic-slice
  271.4 48.1 %all-reduce.1 = f32[128]{0:T(128)S(1)} all-reduce(f32[128]{0:T(128)S(1)} %dynamic-update-slice), channel_id=1, replica_groups=mesh['batch'=32,'row'=4,'col'=4] {'batch'}, use_global_device_ids=true, to_apply=%add.1 | all-reduce | flops 128 | bytes 1024
  319.6 2.0 copy.18
  321.6 3.5 all-to-all-start
  325.1 0.6 gather_fusion.1
  325.8 5.5 %all-to-all-done = bf16[4,64,768]{2,0,1:T(4,128)(2,1)S(1)} async-done(((bf16[4,64,768]{2,0,1:T(4,128)(2,1)}), bf16[4,64,768]{2,0,1:T(4,128)(2,1)S(1)}, u32[]{:S(2)}, u32[]{:S(2)}) %all-to-all-start) | async-done | bytes 393248 | tf_op jit(solution)/shard_map/all_to_all | solution.py:95
  331.3 1.2 copy.26
  332.5 1.5 reshape.109
  334.5 1.4 fusion.46
  336.0 32.3 %all-gather = f32[32,4,1024]{2,1,0:T(4,128)S(1)} all-gather(f32[1,4,1024]{2,1,0:T(4,128)S(1)} %reshape.132), channel_id=1, replica_groups=mesh['batch'=32,'row'=4,'col'=4] {'batch'}, dimensions={0}, use_global_device_ids=true | all-gather | bytes 540672 | tf_op jit(solution)/shard_map/all_gather | solution.py:105
  368.5 0.6 gather_fusion
  369.4 0.7 multiply_add_fusion
  (54 shorter events, 2.4 us)
Async XLA Ops:
  6.5 152.0 %copy-start = (bf16[768,3,384]{2,0,1:T(8,128)(2,1)S(1)}, bf16[768,3,384]{2,0,1:T(8,128)(2,1)}, u32[]{:S(2)}) copy-start(bf16[768,3,384]{2,0,1:T(8,128)(2,1)} %param.16) | copy-start | bytes 5308420
  6.5 6.3 %copy-start.1 = (bf16[4,16,3072]{2,1,0:T(8,128)(2,1)S(1)}, bf16[4,16,3072]{2,1,0:T(8,128)(2,1)}, u32[]{:S(2)}) copy-start(bf16[4,16,3072]{2,1,0:T(8,128)(2,1)} %param.13) | copy-start | bytes 1179652
  6.5 73.0 %all-gather.4.cloned.1.call-start = ((), (), s32[]{:S(2)}) async-start(), calls=%async_computation.2 | async-start | bytes 3342336 | tf_op jit(solution)/shard_map/all_gather | solution.py:62
  11.7 146.9 %all-gather.6.cloned.1.call-start = ((), (), s32[]{:S(2)}) async-start(), calls=%async_computation.3 | async-start | bytes 6684672 | tf_op jit(solution)/shard_map/all_gather | solution.py:61
  14.1 240.5 %all-reduce.5.cloned.1.call-start = ((), (), s32[]{:S(2)}) async-start(), calls=%async_computation.5 | async-start | bytes 6291456 | tf_op jit(solution)/shard_map/psum | solution.py:72
  163.5 0.7 copy-start.9
  163.5 0.7 copy-start.5
  163.6 156.0 %reduce-scatter.2.cloned.1.call-start = ((), (), s32[]{:S(2)}) async-start(), calls=%async_computation.4 | async-start | bytes 1966080 | tf_op jit(solution)/shard_map/reduce_scatter | solution.py:92
  254.6 3.7 copy-start.2
  258.7 1.1 copy-start.3
  263.4 7.7 %copy-start.7 = (f32[4]{0:T(128)S(1)}, f32[4]{0:T(128)}, u32[]{:S(2)}) copy-start(f32[4]{0:T(128)} %param.23) | copy-start | bytes 52
  263.4 56.1 %copy-start.8 = (s32[4]{0:T(128)S(1)}, s32[4]{0:T(128)}, u32[]{:S(2)}) copy-start(s32[4]{0:T(128)} %param.22) | copy-start | bytes 52
  321.6 9.7 %all-to-all-start = ((bf16[4,64,768]{2,0,1:T(4,128)(2,1)}), bf16[4,64,768]{2,0,1:T(4,128)(2,1)S(1)}, u32[]{:S(2)}, u32[]{:S(2)}) async-start(bf16[4,64,768]{2,0,1:T(4,128)(2,1)} %copy.18), calls=%async_computation.1 | async-start | bytes 786432 | tf_op jit(solution)/shard_map/all_to_all | solution.py:95
  334.2 35.1 %copy-start.4 = (f32[4,16,64]{2,1,0:T(8,128)S(1)}, f32[4,16,64]{2,1,0:T(8,128)}, u32[]{:S(2)}) copy-start(f32[4,16,64]{2,1,0:T(8,128)} %param.25) | copy-start | bytes 49156
  334.2 35.1 %copy-start.6 = (f32[4]{0:T(128)S(1)}, f32[4]{0:T(128)}, u32[]{:S(2)}) copy-start(f32[4]{0:T(128)} %param.24) | copy-start | bytes 52
Sparse Core Ops, SparseCore 0:
  11.8 67.7 all-gather.3
  82.6 75.8 all-gather.5
  163.7 90.8 all-reduce.4
  269.3 32.5 reduce-scatter.1
where the time goes:
time: 377 us
  waiting for transfers between devices  237 us (63%)
  blocking collectives  80.4 us (21%)
  matrix products  18.2 us (5%)
  between operations  14 us (4%)
  other arithmetic  12.5 us (3%)
  local copies, waits for them, and re-layouts  10.9 us (3%)
    psum x1, waiting for transfers between devices, per_device(): lax.psum(qkv_term.astype(jnp.bfloat16), 'col').astype(jnp.float32)  90.3 us
    all_gather x1, waiting for transfers between devices, per_device(): lax.all_gather(image_mod, ('row', 'col'), axis=1, tiled=True)  75.8 us
    all_gather x1, waiting for transfers between devices, per_device(): lax.all_gather(text_mod, ('row', 'col'), axis=1, tiled=True)  65.4 us
    unnamed x1, blocking collectives  48.1 us
    all_gather x1, blocking collectives, per_device(): lax.all_gather(flat_velocity, 'batch', axis=0, tiled=True)  32.3 us
  transfers between devices with their start and end apart: 5, of which 4 were waited for; matrix products, arithmetic and copies ran while one was open for 2% of the time, Pallas kernels for 0%

commit v1 on v0

--- a/solution.py
+++ b/solution.py
@@ -1,3 +1,4 @@
+import functools
 import math
 import jax
 import jax.numpy as jnp
@@ -5,6 +6,14 @@
 from jax.sharding import PartitionSpec as P
 
 epsilon = 1e-06
+
+
+def attach_outputs_in(xin, axis_id):
+    right_arr = lax.all_gather(xin, axis_name=axis_id)
+    return jnp.sum(right_arr, axis=0)
+
+
+put_the_slabs = functools.partial(attach_outputs_in, axis_id="col")
 
 
 def layer_norm(values):
@@ -69,7 +78,7 @@
     )
     kv_term = jnp.einsum("std,dhe->sthe", text_all, kv_weight, preferred_element_type=jnp.float32)
     qkv_sum, kv_sum = (
-        lax.psum(qkv_term.astype(jnp.bfloat16), "col").astype(jnp.float32),
+        put_the_slabs(qkv_term.astype(jnp.bfloat16)).astype(jnp.float32),
         lax.psum(kv_term.astype(jnp.bfloat16), "col").astype(jnp.float32),
     )
     queries = head_norm(qkv_sum[..., :head_size], norm_gains[0]).astype(jnp.bfloat16)

time: 377 us -> 451 us (1.20)
  waiting for transfers between devices: 237 us -> 302 us
  other arithmetic: 12.5 us -> 23 us
    all_gather x0 -> x1, waiting for transfers between devices: none -> 101 us  [attach_outputs_in(): right_arr = lax.all_gather(xin, axis_name=axis_id)]
    psum x1, waiting for transfers between devices: 90.3 us -> 54.4 us  [per_device(): lax.psum(kv_term.astype(jnp.bfloat16), 'col').astype(jnp.float32)]
    reduce_sum x0 -> x1, other arithmetic: none -> 7.34 us  [attach_outputs_in(): return jnp.sum(right_arr, axis=0)]
  transfers between devices with their start and end apart: 5 -> 6, of which waited for: 4 -> 5; matrix products, arithmetic and copies ran while one was open for 2% -> 4% of each run, Pallas kernels for 0% -> 0%
where the time goes in v1:
time: 451 us; the launch traced here: 450 us
  waiting for transfers between devices  302 us (67%)
  blocking collectives  80.4 us (18%)
  other arithmetic  23 us (5%)
  matrix products  18.1 us (4%)
  between operations  14 us (3%)
  local copies, waits for them, and re-layouts  8.47 us (2%)
    all_gather x1, waiting for transfers between devices, attach_outputs_in(): right_arr = lax.all_gather(xin, axis_name=axis_id)  101 us
    all_gather x1, waiting for transfers between devices, per_device(): lax.all_gather(image_mod, ('row', 'col'), axis=1, tiled=True)  75.7 us
    all_gather x1, waiting for transfers between devices, per_device(): lax.all_gather(text_mod, ('row', 'col'), axis=1, tiled=True)  65.4 us
    psum x1, waiting for transfers between devices, per_device(): lax.psum(kv_term.astype(jnp.bfloat16), 'col').astype(jnp.float32)  54.4 us
    unnamed x1, blocking collectives  48 us
    all_gather x1, blocking collectives, per_device(): lax.all_gather(flat_velocity, 'batch', axis=0, tiled=True)  32.4 us
  transfers between devices with their start and end apart: 6, of which 5 were waited for; matrix products, arithmetic and copies ran while one was open for 4% of the time, Pallas kernels for 0%

profile of v1, /device:TPU:1, one launch (start us, length us, event | category | flops | bytes accessed | tf_op | source)
XLA Modules:
  0.0 450.0 jit_solution(8894481704465383309)
XLA Ops:
  6.5 1.2 convert_reduce_fusion.1
  7.7 1.1 fusion.42
  8.9 1.0 slice_bitcast_fusion.3
  9.9 1.7 fusion.45
  11.7 1.1 convert_reduce_fusion
  13.1 1.0 fusion.30
  14.1 65.4 %all-gather.6.cloned.1.call-done = bf16[4,128,3072]{2,1,0:T(8,128)(2,1)} async-done(((bf16[4,8,3072]{2,1,0:T(8,128)(2,1)}), bf16[4,128,3072]{2,1,0:T(8,128)(2,1)}) %all-gather.6.cloned.1.call-update) | async-done | bytes 3145744 | tf_op jit(solution)/shard_map/all_gather | solution.py:71
  79.5 3.2 convolution_convert_fusion.1
  82.8 75.7 %all-gather.8.cloned.1.call-done = bf16[4,256,3072]{2,1,0:T(8,128)(2,1)} async-done(((bf16[4,16,3072]{2,1,0:T(8,128)(2,1)}), bf16[4,256,3072]{2,1,0:T(8,128)(2,1)}) %all-gather.8.cloned.1.call-update) | async-done | bytes 6291472 | tf_op jit(solution)/shard_map/all_gather | solution.py:70
  158.5 5.0 %convolution_convert_fusion = bf16[4,256,3,384]{3,1,2,0:T(8,128)(2,1)} fusion(bf16[768,3,384]{2,0,1:T(8,128)(2,1)S(1)} %copy-done, bf16[4,256,3072]{2,1,0:T(8,128)(2,1)} %all-gather.8.cloned.1.call-done, s32[]{:T(128)S(6)} %select_n.32), kind=kOutput, calls=%fused_computation.9 | convolution fusion | flops 1813118976 | bytes 5701636 | tf_op jit(solution)/shard_map/std,dhe->sthe/dot_general | solution.py:76
  163.6 0.6 copy-done.8
  164.3 54.4 %all-reduce.4.cloned.1.call-done = bf16[4,128,3,256]{3,1,2,0:T(8,128)(2,1)} async-done(((bf16[4,128,3,256]{3,1,2,0:T(8,128)(2,1)}), bf16[4,128,3,256]{3,1,2,0:T(8,128)(2,1)}) %all-reduce.4.cloned.1.call-update) | async-done | bytes 786448 | tf_op jit(solution)/shard_map/psum | solution.py:82
  218.7 1.3 fusion.31
  220.0 2.0 fusion.33
  222.0 101.0 %all-gather.10.cloned.1.call-done = bf16[16,256,3,384]{3,1,2,0:T(8,128)(2,1)} async-done(((bf16[4,256,3,384]{3,1,2,0:T(8,128)(2,1)}), bf16[16,256,3,384]{3,1,2,0:T(8,128)(2,1)}) %all-gather.10.cloned.1.call-update) | async-done | bytes 9437200 | tf_op jit(solution)/shard_map/all_gather | solution.py:12
  322.9 7.3 %reduce_sum.124 = bf16[4,256,3,384]{3,1,2,0:T(8,128)(2,1)} reduce(bf16[4,4,256,3,384]{4,2,3,1,0:T(8,128)(2,1)} %bitcast.59, bf16[]{:T(256)} %constant.77.clone.1), dimensions={0}, to_apply=%region_5.0 | reduce | flops 3538944 | bytes 11796482 | tf_op jit(solution)/shard_map/reduce_sum | solution.py:13
  330.3 2.1 convert_element_type.67
  332.4 0.9 multiply_reduce_fusion.1
  333.9 2.8 fusion
  336.7 5.7 %bitcast_convert_fusion = bf16[4,256,768]{2,1,0:T(8,128)(2,1)} fusion(f32[4,3,256,384]{3,2,1,0:T(8,128)} %get-tuple-element.23, f32[4,384]{1,0:T(4,128)S(1)} %pad_convert_fusion, bf16[4,256,3,128]{3,1,2,0:T(8,128)(2,1)S(1)} %slice-done, bf16[4,128,3,128]{3,1,2,0:T(8,128)(2,1)S(1)} %slice-done.1, f32[4,256,3]{1,2,0:T(4,128)S(1)} %bitcast.62, ...), kind=kOutput, calls=%fused_computation.5 | convolution fusion | flops 913440768 | bytes 8079360 | tf_op jit(solution)/shard_map/sqhe,hed->sqd/dot_general | solution.py:100
  342.5 1.3 dynamic-slice
  344.7 48.0 %all-reduce.1 = f32[128]{0:T(128)S(1)} all-reduce(f32[128]{0:T(128)S(1)} %dynamic-update-slice), channel_id=1, replica_groups=mesh['batch'=32,'row'=4,'col'=4] {'batch'}, use_global_device_ids=true, to_apply=%add.1 | all-reduce | flops 128 | bytes 1024
  392.7 2.0 copy.18
  394.7 3.7 all-to-all-start
  398.4 0.6 gather_fusion.1
  399.1 5.6 %all-to-all-done = bf16[4,64,768]{2,0,1:T(4,128)(2,1)S(1)} async-done(((bf16[4,64,768]{2,0,1:T(4,128)(2,1)}), bf16[4,64,768]{2,0,1:T(4,128)(2,1)S(1)}, u32[]{:S(2)}, u32[]{:S(2)}) %all-to-all-start) | async-done | bytes 393248 | tf_op jit(solution)/shard_map/all_to_all | solution.py:104
  404.6 1.2 copy.26
  405.8 1.5 reshape.109
  407.8 1.4 fusion.46
  409.3 32.4 %all-gather.1 = f32[32,4,1024]{2,1,0:T(4,128)S(1)} all-gather(f32[1,4,1024]{2,1,0:T(4,128)S(1)} %reshape.133), channel_id=1, replica_groups=mesh['batch'=32,'row'=4,'col'=4] {'batch'}, dimensions={0}, use_global_device_ids=true | all-gather | bytes 540672 | tf_op jit(solution)/shard_map/all_gather | solution.py:114
  441.9 0.6 gather_fusion
  442.8 0.7 multiply_add_fusion
  (59 shorter events, 2.4 us)
Async XLA Ops:
  6.5 152.0 %copy-start = (bf16[768,3,384]{2,0,1:T(8,128)(2,1)S(1)}, bf16[768,3,384]{2,0,1:T(8,128)(2,1)}, u32[]{:S(2)}) copy-start(bf16[768,3,384]{2,0,1:T(8,128)(2,1)} %param.16) | copy-start | bytes 5308420
  6.5 6.3 %copy-start.1 = (bf16[4,16,3072]{2,1,0:T(8,128)(2,1)S(1)}, bf16[4,16,3072]{2,1,0:T(8,128)(2,1)}, u32[]{:S(2)}) copy-start(bf16[4,16,3072]{2,1,0:T(8,128)(2,1)} %param.13) | copy-start | bytes 1179652
  6.5 73.0 %all-gather.6.cloned.1.call-start = ((), (), s32[]{:S(2)}) async-start(), calls=%async_computation.2 | async-start | bytes 3342336 | tf_op jit(solution)/shard_map/all_gather | solution.py:71
  11.6 146.9 %all-gather.8.cloned.1.call-start = ((), (), s32[]{:S(2)}) async-start(), calls=%async_computation.4 | async-start | bytes 6684672 | tf_op jit(solution)/shard_map/all_gather | solution.py:70
  14.1 204.6 %all-reduce.4.cloned.1.call-start = ((), (), s32[]{:S(2)}) async-start(), calls=%async_computation.3 | async-start | bytes 1572864 | tf_op jit(solution)/shard_map/psum | solution.py:82
  82.8 240.2 %all-gather.10.cloned.1.call-start = ((), (), s32[]{:S(2)}) async-start(), calls=%async_computation.6 | async-start | bytes 11796480 | tf_op jit(solution)/shard_map/all_gather | solution.py:12
  163.5 0.7 copy-start.8
  163.5 0.7 copy-start.4
  163.5 229.1 %reduce-scatter.2.cloned.1.call-start = ((), (), s32[]{:S(2)}) async-start(), calls=%async_computation.5 | async-start | bytes 1966080 | tf_op jit(solution)/shard_map/reduce_scatter | solution.py:101
  332.4 1.4 copy-start.2
  333.9 2.8 slice-start
  333.9 2.8 slice-start.1
  336.7 7.7 %copy-start.6 = (f32[4]{0:T(128)S(1)}, f32[4]{0:T(128)}, u32[]{:S(2)}) copy-start(f32[4]{0:T(128)} %param.23) | copy-start | bytes 52
  336.7 55.9 %copy-start.7 = (s32[4]{0:T(128)S(1)}, s32[4]{0:T(128)}, u32[]{:S(2)}) copy-start(s32[4]{0:T(128)} %param.22) | copy-start | bytes 52
  394.7 9.9 %all-to-all-start = ((bf16[4,64,768]{2,0,1:T(4,128)(2,1)}), bf16[4,64,768]{2,0,1:T(4,128)(2,1)S(1)}, u32[]{:S(2)}, u32[]{:S(2)}) async-start(bf16[4,64,768]{2,0,1:T(4,128)(2,1)} %copy.18), calls=%async_computation.1 | async-start | bytes 786432 | tf_op jit(solution)/shard_map/all_to_all | solution.py:104
  407.6 35.2 %copy-start.3 = (f32[4,16,64]{2,1,0:T(8,128)S(1)}, f32[4,16,64]{2,1,0:T(8,128)}, u32[]{:S(2)}) copy-start(f32[4,16,64]{2,1,0:T(8,128)} %param.25) | copy-start | bytes 49156
  407.6 35.2 %copy-start.5 = (f32[4]{0:T(128)S(1)}, f32[4]{0:T(128)}, u32[]{:S(2)}) copy-start(f32[4]{0:T(128)} %param.24) | copy-start | bytes 52
Sparse Core Ops, SparseCore 0:
  11.8 67.7 all-gather.5
  82.6 75.8 all-gather.7
  160.9 57.7 all-reduce.3
  220.6 102.2 all-gather.9
  342.6 33.7 reduce-scatter.1
